TPU v7x, 256 devices: a whole 4x4x8 slice. The times are simulated.
256 devices in a mesh: obs: 4 (over x), bfly: 64 (over z, y, core).
Axes of the slice: x: 4, y: 4, z: 8, core: 2. Of those that a mesh axis runs over, the one named last changes fastest.
Arguments:
- obs_field: float32 [262144, 1024], P(('obs', 'bfly')), may hold values from -6 to 6
- observer_leaf_bases: float32 [512, 512, 256], P(('obs', 'bfly')), may hold values from -0.25 to 0.25
- transfer: float32 [4, 512, 256, 512], P(None, ('obs', 'bfly')), may hold values from -0.25 to 0.25
- src_basis: float32 [128, 512, 256], P('bfly'), may hold values from -0.375 to 0.375
- leaf_map: int32 [4, 64], replicated, may hold values from 0 to 3, as said below
- partner_perm: int32 [4, 256], replicated, may hold values from 0 to 255, each once within a row
Outputs:
- src_field: float32 [1024, 65536], P('obs', 'bfly')
Inputs may be any that keep to these rules, and one draw needn't show every extreme that they name: In every column b, leaf_map[o, b] = (o + r_b) mod 4 for one offset r_b of that column, so each column names every observer group once. `partner_perm`: each row is a permutation of the rank indices.
All inputs are finite; a program needn't handle non-finite values.
Results may differ from a plain program's by a relative error of at most 0.0001.
Values sent between devices are 32-bit elements; how exact they have to be, the bound alone decides.
No kernel may reach another device: no remote copies, remote signals or barrier semaphores. Data moves between devices by JAX's collectives and lax.ppermute only.
A program may use at most 64 MiB of HBM per device.

v0:
```python
import jax
import jax.numpy as jnp
from jax import lax
from jax.sharding import PartitionSpec as P


def swapped(block, axis, apart):
    count = lax.axis_size(axis)
    route = []
    for low in range(count):
        high = low | 1 << apart
        if high != low and high < count:
            route += [(low, high), (high, low)]
    return lax.ppermute(block, axis, route)


def body(obs_field, observer_leaf_bases, transfer, src_basis, leaf_map, partner_perm):
    highest_level = lax.Precision.HIGHEST
    node_count, leaf_rows, rank_size = observer_leaf_bases.shape
    col_count = obs_field.shape[1]
    level_count = transfer.shape[0]
    n_groups = lax.axis_size("obs")
    obs_index = lax.axis_index("obs")
    bfly_index = lax.axis_index("bfly")
    block_list = obs_field.reshape(node_count, leaf_rows, col_count)
    projected_field = jnp.einsum(
        "jlr,jlc->jrc",
        observer_leaf_bases,
        block_list,
        precision=highest_level,
        preferred_element_type=jnp.float32,
    )
    source = leaf_map[obs_index, bfly_index]
    block_rows = node_count * rank_size
    flattened = projected_field.reshape(block_rows, col_count)
    target = source * block_rows
    shards = lax.all_gather(flattened, "obs", axis=0, tiled=True)
    first_row = jnp.int32(0)
    row_count = shards.shape[0]
    offset = jnp.clip(target, 0, row_count - block_rows)
    sliced_rows = lax.dynamic_slice_in_dim(shards, offset, block_rows, 0)
    inside = jnp.logical_and(target >= first_row, target < first_row + row_count)
    gathered = jnp.where(inside, sliced_rows, jnp.zeros_like(flattened))
    carried = gathered.reshape(node_count, rank_size, col_count)
    rank_index_list = jnp.arange(rank_size, dtype=jnp.int32)
    for level_index in range(level_count):
        partner = swapped(carried, "bfly", level_index)
        perm_row = partner_perm[level_index]
        onehot = (perm_row[:, None] == rank_index_list[None, :]).astype(jnp.float32)
        level_mats = transfer[level_index]
        own_part = level_mats[:, :, :rank_size]
        far_part = jnp.einsum(
            "jri,im->jrm",
            level_mats[:, :, rank_size:],
            onehot,
            precision=highest_level,
            preferred_element_type=jnp.float32,
        )
        own_term = jnp.einsum(
            "jrs,jsc->jrc",
            own_part,
            carried,
            precision=highest_level,
            preferred_element_type=jnp.float32,
        )
        far_term = jnp.einsum(
            "jrs,jsc->jrc",
            far_part,
            partner,
            precision=highest_level,
            preferred_element_type=jnp.float32,
        )
        carried = own_term + far_term
    share_cols = col_count // n_groups
    product = jnp.einsum(
        "jlr,jrc->cjl",
        src_basis,
        carried,
        precision=highest_level,
        preferred_element_type=jnp.float32,
    )
    return lax.psum_scatter(
        product.reshape(share_cols * lax.axis_size("obs"), node_count * leaf_rows),
        "obs",
        scatter_dimension=0,
        tiled=True,
    )


def solution(mesh):
    placed = (
        P(("obs", "bfly"), None),
        P(("obs", "bfly"), None, None),
        P(None, ("obs", "bfly"), None, None),
        P("bfly", None, None),
        P(),
        P(),
    )
    return jax.shard_map(
        body, mesh=mesh, in_specs=placed, out_specs=P("obs", "bfly"), check_vma=False
    )
```

profile of v0, /device:TPU:1, one launch (start us, length us, event | category | flops | bytes accessed | tf_op | source)
XLA Modules:
  0.0 332.2 jit_solution(14697301958873001551)
XLA Ops:
  6.5 0.0 copy-start
  6.5 0.0 all-gather.2.cloned.1.call-start
  6.5 7.6 %fusion.30 = f32[2,256,1024]{2,1,0:T(8,128)} fusion(f32[2,512,256]{2,1,0:T(8,128)} %param.7, f32[2,512,1024]{2,1,0:T(8,128)} %bitcast.70), kind=kOutput, calls=%fused_computation.43 | convolution fusion | flops 3221225472 | bytes 7340032 | tf_op jit(solution)/shard_map/jlr,jlc->jrc/dot_general | solution.py:26
  14.1 0.0 copy-start.2
  14.1 0.0 all-gather.2.cloned.1.call-update
  14.1 0.0 reduce-scatter.2.cloned.1.call-start
  14.2 1.3 dynamic_slice.6
  16.1 87.6 %all-gather.2.cloned.1.call-done = f32[2048,1024]{1,0:T(8,128)} async-done(((f32[512,1024]{1,0:T(8,128)}), f32[2048,1024]{1,0:T(8,128)}) %all-gather.2.cloned.1.call-update) | async-done | bytes 8388624 | tf_op jit(solution)/shard_map/all_gather | solution.py:37
  103.7 0.0 copy-start.1
  103.7 2.0 dynamic-slice_select_fusion
  105.8 0.9 collective-permute-start
  106.7 0.0 copy-done.2
  106.7 0.0 copy-done.1
  106.7 0.4 slice_bitcast_fusion
  107.2 0.5 convolution_bitcast_fusion.2
  107.6 3.5 %fusion.12 = f32[2,1024,256]{2,1,0:T(8,128)S(1)} fusion(f32[2,256,1024]{2,1,0:T(8,128)S(1)} %bitcast.69, f32[2,256,512]{2,1,0:T(8,128)S(1)} %get-tuple-element.7), kind=kOutput, calls=%fused_computation.24 | convolution fusion | flops 1610612736 | bytes 4718592 | tf_op jit(solution)/shard_map/jrs,jsc->jrc/dot_general | solution.py:59
  111.1 0.0 collective-permute-done
  111.1 3.5 %bitcast_add_fusion.4 = f32[2,256,1024]{1,2,0:T(8,128)S(1)} fusion(f32[2,1024,256]{2,1,0:T(8,128)S(1)} %fusion.12, f32[2,256,256]{2,1,0:T(8,128)S(1)} %convolution_bitcast_fusion.2, f32[2,256,1024]{2,1,0:T(8,128)S(1)} %collective-permute-done), kind=kOutput, calls=%fused_computation.4 | convolution fusion | flops 1611137024 | bytes 6815744 | tf_op jit(solution)/shard_map/jrs,jsc->jrc/dot_general | solution.py:66
  114.6 1.5 collective-permute-start.1
  116.2 0.5 convolution_bitcast_fusion.1
  116.6 1.9 fusion.9
  118.6 43.1 %collective-permute-done.1 = f32[2,256,1024]{1,2,0:T(8,128)S(1)} collective-permute-done((f32[2,256,1024]{1,2,0:T(8,128)S(1)}, f32[2,256,1024]{1,2,0:T(8,128)S(1)}, u32[]{:S(2)}, u32[]{:S(2)}) %collective-permute-start.1) | collective-permute-done | bytes 2097184 | tf_op jit(solution)/shard_map/ppermute | solution.py:14
  161.6 2.1 bitcast_add_fusion.3
  163.7 2.8 collective-permute-start.2
  166.6 0.5 convolution_bitcast_fusion
  167.0 1.9 fusion.6
  169.0 42.1 %collective-permute-done.2 = f32[2,256,1024]{1,2,0:T(8,128)S(1)} collective-permute-done((f32[2,256,1024]{1,2,0:T(8,128)S(1)}, f32[2,256,1024]{1,2,0:T(8,128)S(1)}, u32[]{:S(2)}, u32[]{:S(2)}) %collective-permute-start.2) | collective-permute-done | bytes 2097184 | tf_op jit(solution)/shard_map/ppermute | solution.py:14
  211.1 2.0 bitcast_add_fusion.2
  213.1 1.6 collective-permute-start.3
  214.7 0.5 fusion.1
  215.2 0.4 copy.35
  215.6 2.0 fusion.3
  217.6 40.6 %collective-permute-done.3 = f32[2,256,1024]{1,2,0:T(8,128)S(1)} collective-permute-done((f32[2,256,1024]{1,2,0:T(8,128)S(1)}, f32[2,256,1024]{1,2,0:T(8,128)S(1)}, u32[]{:S(2)}, u32[]{:S(2)}) %collective-permute-start.3) | collective-permute-done | bytes 2097184 | tf_op jit(solution)/shard_map/ppermute | solution.py:14
  258.3 3.5 %fusion.14 = f32[2,256,1024]{2,1,0:T(8,128)S(1)} fusion(f32[2,256,1024]{1,2,0:T(8,128)S(1)} %collective-permute-done.3, f32[2,256,256]{1,0,2:T(2,128)S(1)} %bitcast.71), kind=kOutput, calls=%fused_computation.26 | convolution fusion | flops 1610612736 | bytes 4718592 | tf_op jit(solution)/shard_map/jrs,jsc->jrc/dot_general | solution.py:66
  261.8 0.0 copy-done
  261.8 5.1 %fusion = f32[2,1024,512]{1,2,0:T(8,128)} fusion(f32[2,512,256]{2,1,0:T(8,128)S(1)} %copy-done, f32[2,256,1024]{2,1,0:T(8,128)S(1)} %fusion.14, f32[2,1024,256]{1,2,0:T(8,128)S(1)} %fusion.3), kind=kOutput, calls=%fused_computation.1 | convolution fusion | flops 3221749760 | bytes 9437184 | tf_op jit(solution)/shard_map/jlr,jrc->cjl/dot_general | solution.py:75
  266.9 5.4 %copy.22 = f32[1024,1024]{1,0:T(8,128)} copy(f32[1024,1024]{0,1:T(8,128)} %bitcast.66) | data formatting | bytes 8388608 | tf_op jit(solution)/shard_map/reshape | solution.py:83
  272.3 0.0 reduce-scatter.2.cloned.1.call-update
  272.3 53.1 %reduce-scatter.2.cloned.1.call-done = f32[256,1024]{1,0:T(8,128)} async-done(((f32[1024,1024]{1,0:T(8,128)}), f32[256,1024]{1,0:T(8,128)}) %reduce-scatter.2.cloned.1.call-update) | async-done | bytes 1048592 | tf_op jit(solution)/shard_map/reduce_scatter | solution.py:82
  (1 shorter events, 0.0 us)
Async XLA Ops:
  6.5 255.2 %copy-start = (f32[2,512,256]{2,1,0:T(8,128)S(1)}, f32[2,512,256]{2,1,0:T(8,128)}, u32[]{:S(2)}) copy-start(f32[2,512,256]{2,1,0:T(8,128)} %param.9) | copy-start | bytes 3145732
  6.5 97.2 %all-gather.2.cloned.1.call-start = ((), (), s32[]{:S(2)}) async-start(), calls=%async_computation.1 | async-start | bytes 10485760 | tf_op jit(solution)/shard_map/all_gather | solution.py:37
  14.1 92.6 %copy-start.2 = (s32[4,256]{1,0:T(4,128)S(1)}, s32[4,256]{1,0:T(4,128)}, u32[]{:S(2)}) copy-start(s32[4,256]{1,0:T(4,128)} %param.11) | copy-start | bytes 12292
  14.1 311.3 %reduce-scatter.2.cloned.1.call-start = ((), (), s32[]{:S(2)}) async-start(), calls=%async_computation.2 | async-start | bytes 5242880 | tf_op jit(solution)/shard_map/reduce_scatter | solution.py:82
  103.7 3.0 copy-start.1
  105.8 5.3 %collective-permute-start = (f32[2,256,1024]{2,1,0:T(8,128)S(1)}, f32[2,256,1024]{2,1,0:T(8,128)S(1)}, u32[]{:S(2)}, u32[]{:S(2)}) collective-permute-start(f32[2,256,1024]{2,1,0:T(8,128)S(1)} %bitcast.68), channel_id=1, source_target_pairs={{0,1},{1,0},{2,3},{3,2},{4,5},{5,4},{6,7},{7,6},{8,9},{9,8},{10,11... | collective-permute-start | bytes 6291464 | tf_op jit(solution)/shard_map/ppermute | solution.py:14
  114.6 47.0 %collective-permute-start.1 = (f32[2,256,1024]{1,2,0:T(8,128)S(1)}, f32[2,256,1024]{1,2,0:T(8,128)S(1)}, u32[]{:S(2)}, u32[]{:S(2)}) collective-permute-start(f32[2,256,1024]{1,2,0:T(8,128)S(1)} %bitcast_add_fusion.4), channel_id=1, source_target_pairs={{0,2},{2,0},{1,3},{3,1},{4,6},{6,4},{5,7},{7,5},{8,10},{10,8},{9,1... | collective-permute-start | bytes 6291464 | tf_op jit(solution)/shard_map/ppermute | solution.py:14
  163.7 47.3 %collective-permute-start.2 = (f32[2,256,1024]{1,2,0:T(8,128)S(1)}, f32[2,256,1024]{1,2,0:T(8,128)S(1)}, u32[]{:S(2)}, u32[]{:S(2)}) collective-permute-start(f32[2,256,1024]{1,2,0:T(8,128)S(1)} %bitcast_add_fusion.3), channel_id=1, source_target_pairs={{0,4},{4,0},{1,5},{5,1},{2,6},{6,2},{3,7},{7,3},{8,12},{12,8},{9,1... | collective-permute-start | bytes 6291464 | tf_op jit(solution)/shard_map/ppermute | solution.py:14
  213.1 45.2 %collective-permute-start.3 = (f32[2,256,1024]{1,2,0:T(8,128)S(1)}, f32[2,256,1024]{1,2,0:T(8,128)S(1)}, u32[]{:S(2)}, u32[]{:S(2)}) collective-permute-start(f32[2,256,1024]{1,2,0:T(8,128)S(1)} %bitcast_add_fusion.2), channel_id=1, source_target_pairs={{0,8},{8,0},{1,9},{9,1},{2,10},{10,2},{3,11},{11,3},{4,12},{12,4},... | collective-permute-start | bytes 6291464 | tf_op jit(solution)/shard_map/ppermute | solution.py:14
Sparse Core Ops, SparseCore 0:
  14.2 89.4 all-gather.1
  272.4 52.9 reduce-scatter.1
where the time goes:
time: 332 us
  waiting for transfers between devices  267 us (80%)
  matrix products  35 us (11%)
  between operations  14.2 us (4%)
  local copies, waits for them, and re-layouts  7.52 us (2%)
  starting transfers between devices  6.95 us (2%)
    ppermute x4, waiting for transfers between devices, swapped(): return lax.ppermute(block, axis, route)  126 us
    all_gather x1, waiting for transfers between devices, body(): shards = lax.all_gather(flattened, 'obs', axis=0, tiled=True)  87.6 us
    reduce_scatter x1, waiting for transfers between devices, body(): lax.psum_scatter(product.reshape(share_cols * lax.axis_size('obs'), node_...  53.1 us
    dot_general x4, matrix products, body(): jnp.einsum('jrs,jsc->jrc', far_part, partner, precision=highest_level, pr...  11.1 us
    dot_general x4, matrix products, body(): jnp.einsum('jrs,jsc->jrc', own_part, carried, precision=highest_level, pr...  9.3 us
    dot_general x1, matrix products, body(): jnp.einsum('jlr,jlc->jrc', observer_leaf_bases, block_list, precision=hig...  7.56 us
    ppermute x4, starting transfers between devices, swapped(): return lax.ppermute(block, axis, route)  6.9 us
  transfers between devices with their start and end apart: 6, of which 5 were waited for; matrix products, arithmetic and copies ran while one was open for 4% of the time, Pallas kernels for 0%

commit v1 on v0

--- a/solution.py
+++ b/solution.py
@@ -34,7 +34,8 @@
     block_rows = node_count * rank_size
     flattened = projected_field.reshape(block_rows, col_count)
     target = source * block_rows
-    shards = lax.all_gather(flattened, "obs", axis=0, tiled=True)
+    sent = jnp.stack([flattened] * lax.axis_size("obs"))
+    shards = jnp.concatenate(lax.all_to_all(sent, "obs", 0, 0), axis=0)
     first_row = jnp.int32(0)
     row_count = shards.shape[0]
     offset = jnp.clip(target, 0, row_count - block_rows)

time: 332 us -> 346 us (1.042)
  starting transfers between devices: 6.95 us -> 16.2 us
  local copies, waits for them, and re-layouts: 7.52 us -> 11.8 us
    all_to_all x0 -> x1, waiting for transfers between devices: none -> 89.8 us  [body(): shards = jnp.concatenate(lax.all_to_all(sent, 'obs', 0, 0), axis=0)]
    all_gather x1 -> x0, waiting for transfers between devices: 87.6 us -> none  [body(): shards = lax.all_gather(flattened, 'obs', axis=0, tiled=True)]
    all_to_all x0 -> x1, starting transfers between devices: none -> 5.76 us  [body(): shards = jnp.concatenate(lax.all_to_all(sent, 'obs', 0, 0), axis=0)]
    another operation x0 -> x1, local copies, waits for them, and re-layouts: none -> 4.3 us  [body(): sent = jnp.stack([flattened] * lax.axis_size('obs'))]
    ppermute x4, starting transfers between devices: 6.9 us -> 10.4 us  [swapped(): return lax.ppermute(block, axis, route)]
where the time goes in v1:
time: 346 us
  waiting for transfers between devices  268 us (77%)
  matrix products  33.9 us (10%)
  starting transfers between devices  16.2 us (5%)
  between operations  14.2 us (4%)
  local copies, waits for them, and re-layouts  11.8 us (3%)
    ppermute x4, waiting for transfers between devices, swapped(): return lax.ppermute(block, axis, route)  125 us
    all_to_all x1, waiting for transfers between devices, body(): shards = jnp.concatenate(lax.all_to_all(sent, 'obs', 0, 0), axis=0)  89.8 us
    reduce_scatter x1, waiting for transfers between devices, body(): lax.psum_scatter(product.reshape(share_cols * lax.axis_size('obs'), node_...  53 us
    dot_general x4, matrix products, body(): jnp.einsum('jrs,jsc->jrc', far_part, partner, precision=highest_level, pr...  11.1 us
    ppermute x4, starting transfers between devices, swapped(): return lax.ppermute(block, axis, route)  10.4 us
    dot_general x4, matrix products, body(): jnp.einsum('jrs,jsc->jrc', own_part, carried, precision=highest_level, pr...  9.44 us
  transfers between devices with their start and end apart: 6, of which 5 were waited for; matrix products, arithmetic and copies ran while one was open for 4% of the time, Pallas kernels for 0%

profile of v1, /device:TPU:1, one launch (start us, length us, event | category | flops | bytes accessed | tf_op | source)
XLA Modules:
  0.0 345.9 jit_solution(9526779768448589648)
XLA Ops:
  6.5 0.0 copy-start
  6.5 6.4 %fusion.30 = f32[2,256,1024]{2,1,0:T(8,128)S(1)} fusion(f32[2,512,256]{2,1,0:T(8,128)} %param.7, f32[2,512,1024]{2,1,0:T(8,128)} %bitcast.71), kind=kOutput, calls=%fused_computation.43 | convolution fusion | flops 3221225472 | bytes 7340032 | tf_op jit(solution)/shard_map/jlr,jlc->jrc/dot_general | solution.py:26
  13.0 4.3 %stack.3 = f32[4,512,1024]{2,1,0:T(8,128)} broadcast(f32[512,1024]{1,0:T(8,128)S(1)} %bitcast.68), dimensions={1,2} | broadcast | bytes 10485760 | tf_op jit(solution)/shard_map/stack | solution.py:37
  17.3 0.0 copy-start.2
  17.3 5.8 %all-to-all-start = ((f32[4,512,1024]{2,1,0:T(8,128)}), f32[4,512,1024]{2,1,0:T(8,128)}, u32[]{:S(2)}, u32[]{:S(2)}) async-start(f32[4,512,1024]{2,1,0:T(8,128)} %stack.3), calls=%async_computation | async-start | bytes 16777216 | tf_op jit(solution)/shard_map/all_to_all | solution.py:38
  23.0 0.0 reduce-scatter.2.cloned.1.call-start
  23.1 1.3 dynamic_slice.6
  25.0 89.8 %all-to-all-done = f32[4,512,1024]{2,1,0:T(8,128)} async-done(((f32[4,512,1024]{2,1,0:T(8,128)}), f32[4,512,1024]{2,1,0:T(8,128)}, u32[]{:S(2)}, u32[]{:S(2)}) %all-to-all-start) | async-done | bytes 8388640 | tf_op jit(solution)/shard_map/all_to_all | solution.py:38
  114.8 0.0 copy-start.1
  114.8 2.0 dynamic-slice_select_fusion
  116.9 3.6 %collective-permute-start = (f32[2,256,1024]{2,1,0:T(8,128)S(1)}, f32[2,256,1024]{2,1,0:T(8,128)S(1)}, u32[]{:S(2)}, u32[]{:S(2)}) collective-permute-start(f32[2,256,1024]{2,1,0:T(8,128)S(1)} %bitcast.69), channel_id=1, source_target_pairs={{0,1},{1,0},{2,3},{3,2},{4,5},{5,4},{6,7},{7,6},{8,9},{9,8},{10,11... | collective-permute-start | bytes 6291464 | tf_op jit(solution)/shard_map/ppermute | solution.py:14
  120.5 0.0 copy-done.2
  120.5 0.0 copy-done.1
  120.5 0.4 slice_bitcast_fusion
  121.0 0.5 convolution_bitcast_fusion.2
  121.4 3.5 fusion.12
  124.9 0.0 collective-permute-done
  124.9 3.5 %bitcast_add_fusion.4 = f32[2,256,1024]{1,2,0:T(8,128)S(1)} fusion(f32[2,1024,256]{2,1,0:T(8,128)S(1)} %fusion.12, f32[2,256,256]{2,1,0:T(8,128)S(1)} %convolution_bitcast_fusion.2, f32[2,256,1024]{2,1,0:T(8,128)S(1)} %collective-permute-done), kind=kOutput, calls=%fused_computation.4 | convolution fusion | flops 1611137024 | bytes 6815744 | tf_op jit(solution)/shard_map/jrs,jsc->jrc/dot_general | solution.py:67
  128.4 1.8 collective-permute-start.1
  130.2 0.5 convolution_bitcast_fusion.1
  130.7 2.0 fusion.9
  132.7 42.6 %collective-permute-done.1 = f32[2,256,1024]{1,2,0:T(8,128)S(1)} collective-permute-done((f32[2,256,1024]{1,2,0:T(8,128)S(1)}, f32[2,256,1024]{1,2,0:T(8,128)S(1)}, u32[]{:S(2)}, u32[]{:S(2)}) %collective-permute-start.1) | collective-permute-done | bytes 2097184 | tf_op jit(solution)/shard_map/ppermute | solution.py:14
  175.3 2.1 bitcast_add_fusion.3
  177.4 3.1 collective-permute-start.2
  180.4 0.5 convolution_bitcast_fusion
  180.9 2.0 fusion.6
  182.9 41.7 %collective-permute-done.2 = f32[2,256,1024]{1,2,0:T(8,128)S(1)} collective-permute-done((f32[2,256,1024]{1,2,0:T(8,128)S(1)}, f32[2,256,1024]{1,2,0:T(8,128)S(1)}, u32[]{:S(2)}, u32[]{:S(2)}) %collective-permute-start.2) | collective-permute-done | bytes 2097184 | tf_op jit(solution)/shard_map/ppermute | solution.py:14
  224.6 2.1 bitcast_add_fusion.2
  226.7 1.9 collective-permute-start.3
  228.6 0.5 fusion.1
  229.1 0.4 copy.35
  229.5 2.0 fusion.3
  231.5 40.5 %collective-permute-done.3 = f32[2,256,1024]{1,2,0:T(8,128)S(1)} collective-permute-done((f32[2,256,1024]{1,2,0:T(8,128)S(1)}, f32[2,256,1024]{1,2,0:T(8,128)S(1)}, u32[]{:S(2)}, u32[]{:S(2)}) %collective-permute-start.3) | collective-permute-done | bytes 2097184 | tf_op jit(solution)/shard_map/ppermute | solution.py:14
  272.0 3.5 %fusion.14 = f32[2,256,1024]{2,1,0:T(8,128)S(1)} fusion(f32[2,256,1024]{1,2,0:T(8,128)S(1)} %collective-permute-done.3, f32[2,256,256]{1,0,2:T(2,128)S(1)} %bitcast.72), kind=kOutput, calls=%fused_computation.26 | convolution fusion | flops 1610612736 | bytes 4718592 | tf_op jit(solution)/shard_map/jrs,jsc->jrc/dot_general | solution.py:67
  275.4 0.0 copy-done
  275.4 5.1 %fusion = f32[2,1024,512]{1,2,0:T(8,128)} fusion(f32[2,512,256]{2,1,0:T(8,128)S(1)} %copy-done, f32[2,256,1024]{2,1,0:T(8,128)S(1)} %fusion.14, f32[2,1024,256]{1,2,0:T(8,128)S(1)} %fusion.3), kind=kOutput, calls=%fused_computation.1 | convolution fusion | flops 3221749760 | bytes 9437184 | tf_op jit(solution)/shard_map/jlr,jrc->cjl/dot_general | solution.py:76
  280.6 5.4 %copy.22 = f32[1024,1024]{1,0:T(8,128)} copy(f32[1024,1024]{0,1:T(8,128)} %bitcast.67) | data formatting | bytes 8388608 | tf_op jit(solution)/shard_map/reshape | solution.py:84
  286.0 0.0 reduce-scatter.2.cloned.1.call-update
  286.0 53.0 %reduce-scatter.2.cloned.1.call-done = f32[256,1024]{1,0:T(8,128)} async-done(((f32[1024,1024]{1,0:T(8,128)}), f32[256,1024]{1,0:T(8,128)}) %reduce-scatter.2.cloned.1.call-update) | async-done | bytes 1048592 | tf_op jit(solution)/shard_map/reduce_scatter | solution.py:83
  (1 shorter events, 0.0 us)
Async XLA Ops:
  6.5 268.9 %copy-start = (f32[2,512,256]{2,1,0:T(8,128)S(1)}, f32[2,512,256]{2,1,0:T(8,128)}, u32[]{:S(2)}) copy-start(f32[2,512,256]{2,1,0:T(8,128)} %param.9) | copy-start | bytes 3145732
  17.3 103.2 %copy-start.2 = (s32[4,256]{1,0:T(4,128)S(1)}, s32[4,256]{1,0:T(4,128)}, u32[]{:S(2)}) copy-start(s32[4,256]{1,0:T(4,128)} %param.11) | copy-start | bytes 12292
  17.3 97.6 %all-to-all-start = ((f32[4,512,1024]{2,1,0:T(8,128)}), f32[4,512,1024]{2,1,0:T(8,128)}, u32[]{:S(2)}, u32[]{:S(2)}) async-start(f32[4,512,1024]{2,1,0:T(8,128)} %stack.3), calls=%async_computation | async-start | bytes 16777216 | tf_op jit(solution)/shard_map/all_to_all | solution.py:38
  23.0 316.0 %reduce-scatter.2.cloned.1.call-start = ((), (), s32[]{:S(2)}) async-start(), calls=%async_computation.2 | async-start | bytes 5242880 | tf_op jit(solution)/shard_map/reduce_scatter | solution.py:83
  114.8 5.7 %copy-start.1 = (f32[4,2,256,512]{3,2,1,0:T(8,128)S(1)}, f32[4,2,256,512]{3,2,1,0:T(8,128)}, u32[]{:S(2)}) copy-start(f32[4,2,256,512]{3,2,1,0:T(8,128)} %param.8) | copy-start | bytes 12582916
  116.9 8.0 %collective-permute-start = (f32[2,256,1024]{2,1,0:T(8,128)S(1)}, f32[2,256,1024]{2,1,0:T(8,128)S(1)}, u32[]{:S(2)}, u32[]{:S(2)}) collective-permute-start(f32[2,256,1024]{2,1,0:T(8,128)S(1)} %bitcast.69), channel_id=1, source_target_pairs={{0,1},{1,0},{2,3},{3,2},{4,5},{5,4},{6,7},{7,6},{8,9},{9,8},{10,11... | collective-permute-start | bytes 6291464 | tf_op jit(solution)/shard_map/ppermute | solution.py:14
  128.4 46.9 %collective-permute-start.1 = (f32[2,256,1024]{1,2,0:T(8,128)S(1)}, f32[2,256,1024]{1,2,0:T(8,128)S(1)}, u32[]{:S(2)}, u32[]{:S(2)}) collective-permute-start(f32[2,256,1024]{1,2,0:T(8,128)S(1)} %bitcast_add_fusion.4), channel_id=1, source_target_pairs={{0,2},{2,0},{1,3},{3,1},{4,6},{6,4},{5,7},{7,5},{8,10},{10,8},{9,1... | collective-permute-start | bytes 6291464 | tf_op jit(solution)/shard_map/ppermute | solution.py:14
  177.4 47.3 %collective-permute-start.2 = (f32[2,256,1024]{1,2,0:T(8,128)S(1)}, f32[2,256,1024]{1,2,0:T(8,128)S(1)}, u32[]{:S(2)}, u32[]{:S(2)}) collective-permute-start(f32[2,256,1024]{1,2,0:T(8,128)S(1)} %bitcast_add_fusion.3), channel_id=1, source_target_pairs={{0,4},{4,0},{1,5},{5,1},{2,6},{6,2},{3,7},{7,3},{8,12},{12,8},{9,1... | collective-permute-start | bytes 6291464 | tf_op jit(solution)/shard_map/ppermute | solution.py:14
  226.7 45.2 %collective-permute-start.3 = (f32[2,256,1024]{1,2,0:T(8,128)S(1)}, f32[2,256,1024]{1,2,0:T(8,128)S(1)}, u32[]{:S(2)}, u32[]{:S(2)}) collective-permute-start(f32[2,256,1024]{1,2,0:T(8,128)S(1)} %bitcast_add_fusion.2), channel_id=1, source_target_pairs={{0,8},{8,0},{1,9},{9,1},{2,10},{10,2},{3,11},{11,3},{4,12},{12,4},... | collective-permute-start | bytes 6291464 | tf_op jit(solution)/shard_map/ppermute | solution.py:14
Sparse Core Ops, SparseCore 0:
  286.1 52.8 reduce-scatter.1
